TPU v7x, 32 devices: a whole 2x2x4 slice. The times are simulated.
32 devices in a mesh: section: 8 (over z, core), tensor: 2 (over x), replica: 2 (over y).
Axes of the slice: x: 2, y: 2, z: 4, core: 2. Of those that a mesh axis runs over, the one named last changes fastest.
Arguments:
- pool_inputs: bfloat16 [8, 256, 2, 1408], P('section', 'replica', None, 'tensor'), may hold values from -6 to 6
- pool_mixed: bfloat16 [8, 256, 1408], P('section', 'replica'), may hold values from -6 to 6
- crop_ids: int32 [8, 8, 128], P('section', 'replica'), may hold values from 0 to 127
- incoming: bfloat16 [8, 256, 1408], P('section', 'replica', 'tensor'), may hold values from -6 to 6
- loss_grads: bfloat16 [3, 256, 1408], P(None, 'replica', 'tensor'), may hold values from -6 to 6
- w_proj: bfloat16 [8, 2, 1408, 1408], P('section', None, ('tensor', 'replica')), may hold values from -0.109375 to 0.109375
- w_up: bfloat16 [8, 1408, 3072], P('section', None, ('tensor', 'replica')), may hold values from -0.15625 to 0.15625
- w_down: bfloat16 [8, 3072, 1408], P('section', ('tensor', 'replica')), may hold values from -0.109375 to 0.109375
Outputs:
- grad_proj: bfloat16 [8, 2, 1408, 1408], P('section', None, ('tensor', 'replica'))
- grad_up: bfloat16 [8, 1408, 3072], P('section', None, ('tensor', 'replica'))
- grad_down: bfloat16 [8, 3072, 1408], P('section', ('tensor', 'replica'))
- outgoing: bfloat16 [8, 256, 2, 1408], P('section', 'replica', None, 'tensor')
All inputs are finite; a program needn't handle non-finite values.
Results may differ from a plain program's by a relative error of at most 0.02.
Values may be sent and summed in bfloat16 or wider, within the bound.
A program may use at most 128 MiB of HBM per device.

v0:
```python
import jax
import jax.numpy as jnp
from jax import lax
from jax.sharding import PartitionSpec as P

gelu_scale = 0.7978845608
gelu_cubic = 0.044715


def from_partner(value, axis, bit):
    mask = 2**bit
    pairs = [(source, source ^ mask) for source in range(lax.axis_size(axis))]
    return lax.ppermute(value, axis, pairs)


def shifted(x, axis, by):
    devices = lax.axis_size(axis)
    pairs = [(i, i + by) for i in range(devices) if 0 <= i + by < devices]
    return lax.ppermute(x, axis, pairs)


def gelu_pair(pre_gelu):
    inner = gelu_scale * (pre_gelu + gelu_cubic * pre_gelu * pre_gelu * pre_gelu)
    tanh_part = jnp.tanh(inner)
    gelu_value = 0.5 * pre_gelu * (1.0 + tanh_part)
    gelu_slope = 0.5 * (1.0 + tanh_part) + 0.5 * pre_gelu * (
        1.0 - tanh_part * tanh_part
    ) * gelu_scale * (1.0 + 3.0 * gelu_cubic * pre_gelu * pre_gelu)
    return (gelu_value, gelu_slope)


def reflect(block, section_count):
    for bit_number in range(section_count.bit_length() - 1):
        block = from_partner(block, "section", bit_number)
    return block


def body(pool_inputs, pool_mixed, crop_ids, incoming, loss_grads, w_proj, w_up, w_down):
    section_index = lax.axis_index("section")
    section_count = lax.axis_size("section")
    proj_full, up_full, down_full = (
        lax.all_gather(w_proj, "replica", axis=2, tiled=True),
        lax.all_gather(w_up, "replica", axis=2, tiled=True),
        lax.all_gather(w_down, "replica", axis=1, tiled=True),
    )
    proj_local = proj_full[0]
    up_local = up_full[0]
    down_local = down_full[0]
    seed_full, loss_full = (
        lax.all_gather(incoming, "tensor", axis=2, tiled=True),
        lax.all_gather(loss_grads, "tensor", axis=2, tiled=True),
    )
    encoder = section_index < section_count // 2
    decoder_flag = jnp.where(encoder, 0.0, 1.0).astype(jnp.bfloat16)
    skip_mask = jnp.stack([jnp.ones((), jnp.bfloat16), decoder_flag])[None, :, None]
    encoder_weight = jnp.where(encoder, 1.0, 0.0).astype(jnp.float32)
    is_top = section_index == section_count - 1
    tick_count = crop_ids.shape[1]
    upstream = seed_full[0]
    kept_inputs, kept_mixed, kept_active, kept_hidden, kept_grads, kept_upstream = (
        [],
        [],
        [],
        [],
        [],
        [],
    )
    input_grad = None
    for tick_index in range(tick_count):
        picked_rows = crop_ids[0, tick_index]
        inputs = pool_inputs[0][picked_rows] * skip_mask
        mixed_rows = pool_mixed[0][picked_rows]
        pre_gelu = jnp.dot(mixed_rows, up_local, preferred_element_type=jnp.float32)
        gelu_value, gelu_slope = gelu_pair(pre_gelu)
        activated = gelu_value.astype(jnp.bfloat16)
        back_act = jnp.einsum("md,fd->mf", upstream, down_local, preferred_element_type=jnp.float32)
        back_hidden = (back_act * gelu_slope).astype(jnp.bfloat16)
        partial_back = jnp.einsum(
            "mf,df->md", back_hidden, up_local, preferred_element_type=jnp.float32
        )
        back_mixed = upstream.astype(jnp.float32) + lax.psum(partial_back, "tensor")
        mixed_grad = back_mixed.astype(jnp.bfloat16)
        input_grad = jnp.einsum(
            "mj,kij->mki", mixed_grad, proj_local, preferred_element_type=jnp.float32
        ).astype(jnp.bfloat16)
        kept_inputs.append(inputs)
        kept_mixed.append(mixed_rows)
        kept_active.append(activated)
        kept_hidden.append(back_hidden)
        kept_grads.append(mixed_grad)
        kept_upstream.append(upstream)
        if tick_index + 1 < tick_count:
            from_above = shifted(input_grad[:, 0], "section", -1)
            mirrored = reflect(input_grad[:, 1], section_count)
            summed = (
                from_above.astype(jnp.float32) + encoder_weight * mirrored.astype(jnp.float32)
            ).astype(jnp.bfloat16)
            summed = lax.all_gather(summed, "tensor", axis=1, tiled=True)
            upstream = jnp.where(is_top, loss_full[tick_index], summed)
    all_inputs = jnp.concatenate(kept_inputs, axis=0)
    all_mixed = jnp.concatenate(kept_mixed, axis=0)
    all_active = jnp.concatenate(kept_active, axis=0)
    all_hidden = jnp.concatenate(kept_hidden, axis=0)
    all_grads = jnp.concatenate(kept_grads, axis=0)
    all_upstream = jnp.concatenate(kept_upstream, axis=0)
    down_total = jnp.einsum(
        "mf,md->fd", all_active, all_upstream, preferred_element_type=jnp.float32
    )
    up_total = jnp.einsum("md,mf->df", all_mixed, all_hidden, preferred_element_type=jnp.float32)
    proj_total = jnp.einsum(
        "mki,mj->kij", all_inputs, all_grads, preferred_element_type=jnp.float32
    )
    reduced = (
        lax.psum_scatter(
            proj_total[None].astype(jnp.bfloat16), "replica", scatter_dimension=2, tiled=True
        ).astype(jnp.float32),
        lax.psum_scatter(
            up_total[None].astype(jnp.bfloat16), "replica", scatter_dimension=2, tiled=True
        ).astype(jnp.float32),
        lax.psum_scatter(
            down_total[None].astype(jnp.bfloat16), "replica", scatter_dimension=1, tiled=True
        ).astype(jnp.float32),
    )
    return (
        reduced[0].astype(jnp.bfloat16),
        reduced[1].astype(jnp.bfloat16),
        reduced[2].astype(jnp.bfloat16),
        input_grad[None],
    )


def solution(mesh):
    in_specs = (
        P("section", "replica", None, "tensor"),
        P("section", "replica", None),
        P("section", "replica", None),
        P("section", "replica", "tensor"),
        P(None, "replica", "tensor"),
        P("section", None, ("tensor", "replica"), None),
        P("section", None, ("tensor", "replica")),
        P("section", ("tensor", "replica"), None),
    )
    out_specs = (
        P("section", None, ("tensor", "replica"), None),
        P("section", None, ("tensor", "replica")),
        P("section", ("tensor", "replica"), None),
        P("section", "replica", None, "tensor"),
    )
    return jax.shard_map(body, mesh=mesh, in_specs=in_specs, out_specs=out_specs, check_vma=False)
```

profile of v0, /device:TPU:0, one launch (start us, length us, event | category | flops | bytes accessed | tf_op | source)
XLA Modules:
  0.0 637.9 jit_solution(14734872152342492354)
XLA Ops:
  8.8 0.9 gather_fusion.4
  9.7 8.2 %all_gather.24 = bf16[1,128,1408]{1,2,0:T(8,128)(2,1)S(1)} all-gather(bf16[1,128,704]{1,2,0:T(8,128)(2,1)S(1)} %copy-done.23), channel_id=1, replica_groups=mesh['section'=8,'tensor'=2,'replica'=2] {'tensor'}, dimensions={2}, use_global_device_ids=true | all-gather | bytes 540672 | tf_op jit(solution)/shard_map/all_gather | solution.py:50
  17.9 52.6 %all-gather.7.cloned.1.call-done = bf16[1,1408,1536]{2,1,0:T(8,128)(2,1)} async-done(((bf16[1,1408,768]{2,1,0:T(8,128)(2,1)}), bf16[1,1408,1536]{2,1,0:T(8,128)(2,1)}) %all-gather.7.cloned.1.call-update) | async-done | bytes 4325392 | tf_op jit(solution)/shard_map/all_gather | solution.py:43
  70.5 4.0 multiply_convert_fusion.3
  74.5 55.8 %all-gather.5.cloned.1.call-done = bf16[1,1536,1408]{2,1,0:T(8,128)(2,1)} async-done(((bf16[1,768,1408]{2,1,0:T(8,128)(2,1)}), bf16[1,1536,1408]{2,1,0:T(8,128)(2,1)}) %all-gather.5.cloned.1.call-update) | async-done | bytes 4325392 | tf_op jit(solution)/shard_map/all_gather | solution.py:44
  130.3 4.0 fusion.56
  135.0 2.4 fusion.14
  138.9 31.7 %all-reduce.5.cloned.1.call-done = f32[128,1408]{1,0:T(8,128)} async-done(((f32[128,1408]{1,0:T(8,128)}), f32[128,1408]{1,0:T(8,128)}) %all-reduce.5.cloned.1.call-update) | async-done | bytes 720912 | tf_op jit(solution)/shard_map/psum | solution.py:81
  170.5 1.2 add_convert_fusion.3
  171.7 54.4 %all-gather.11.cloned.1.call-done = bf16[1,2,704,1408]{3,2,1,0:T(8,128)(2,1)} async-done(((bf16[1,2,352,1408]{3,2,1,0:T(8,128)(2,1)}), bf16[1,2,704,1408]{3,2,1,0:T(8,128)(2,1)}) %all-gather.11.cloned.1.call-update) | async-done | bytes 3964944 | tf_op jit(solution)/shard_map/all_gather | solution.py:42
  226.1 3.3 fusion.100
  229.6 0.9 gather_fusion.5
  230.9 1.5 collective-permute-start.2
  232.4 16.7 %all-gather.9.cloned.1.call-done = bf16[3,128,1408]{1,2,0:T(8,128)(2,1)} async-done(((bf16[3,128,704]{1,2,0:T(8,128)(2,1)}), bf16[3,128,1408]{1,2,0:T(8,128)(2,1)}) %all-gather.9.cloned.1.call-update) | async-done | bytes 1081360 | tf_op jit(solution)/shard_map/all_gather | solution.py:51
  249.2 1.3 fusion.147
  250.7 1.3 collective-permute-start
  252.0 3.1 collective-permute-start.3
  255.1 4.2 multiply_convert_fusion.2
  259.2 6.9 %collective-permute-done.3 = bf16[128,704]{0,1:T(8,128)(2,1)S(1)} collective-permute-done((bf16[128,704]{0,1:T(8,128)(2,1)S(1)}, bf16[128,704]{0,1:T(8,128)(2,1)S(1)}, u32[]{:S(2)}, u32[]{:S(2)}) %collective-permute-start.3) | collective-permute-done | bytes 180256 | tf_op jit(solution)/shard_map/ppermute | solution.py:13
  266.2 6.2 all_gather.29
  272.7 4.2 fusion.53
  277.7 2.4 fusion.10
  280.1 32.3 %all-reduce.7.cloned.1.call-done = f32[128,1408]{1,0:T(8,128)} async-done(((f32[128,1408]{1,0:T(8,128)}), f32[128,1408]{1,0:T(8,128)}) %all-reduce.7.cloned.1.call-update) | async-done | bytes 720912 | tf_op jit(solution)/shard_map/psum | solution.py:81
  312.4 1.2 add_convert_fusion.2
  313.6 3.5 fusion.103
  317.1 1.4 collective-permute-done.5
  318.6 1.5 collective-permute-start.6
  320.0 0.9 gather_fusion.6
  321.2 1.3 collective-permute-start.4
  322.5 2.7 collective-permute-done.6
  325.1 2.4 collective-permute-start.7
  327.6 4.1 multiply_convert_fusion.1
  331.7 5.0 collective-permute-done.7
  336.7 6.4 %all_gather.30 = bf16[128,1408]{0,1:T(8,128)(2,1)S(1)} all-gather(bf16[128,704]{0,1:T(8,128)(2,1)S(1)} %add_convert_fusion.5), channel_id=1, replica_groups=mesh['section'=8,'tensor'=2,'replica'=2] {'tensor'}, dimensions={1}, use_global_device_ids=true | all-gather | bytes 540672 | tf_op jit(solution)/shard_map/all_gather | solution.py:98
  343.4 4.2 fusion.50
  348.4 2.4 fusion.6
  350.9 32.9 %all-reduce.9.cloned.1.call-done = f32[128,1408]{1,0:T(8,128)} async-done(((f32[128,1408]{1,0:T(8,128)}), f32[128,1408]{1,0:T(8,128)}) %all-reduce.9.cloned.1.call-update) | async-done | bytes 720912 | tf_op jit(solution)/shard_map/psum | solution.py:81
  383.8 1.2 add_convert_fusion.1
  385.0 3.4 fusion.106
  388.5 1.4 collective-permute-done.9
  389.9 1.5 collective-permute-start.10
  391.4 0.9 gather_fusion.7
  392.6 1.3 collective-permute-start.8
  393.9 2.7 collective-permute-done.10
  396.5 2.4 collective-permute-start.11
  399.0 4.1 multiply_convert_fusion
  403.1 5.0 collective-permute-done.11
  408.2 6.2 all_gather.31
  414.6 4.2 fusion.47
  419.6 2.4 fusion.2
  422.9 1.4 gather_fusion
  424.4 1.4 gather_fusion.1
  425.8 1.4 gather_fusion.2
  427.2 1.4 gather_fusion.3
  431.2 1.0 broadcast_multiply_fusion.3
  432.3 22.7 %all-reduce.11.cloned.1.call-done = f32[128,1408]{1,0:T(8,128)} async-done(((f32[128,1408]{1,0:T(8,128)}), f32[128,1408]{1,0:T(8,128)}) %all-reduce.11.cloned.1.call-update) | async-done | bytes 720912 | tf_op jit(solution)/shard_map/psum | solution.py:81
  455.0 1.3 add_convert_fusion
  456.3 5.7 fusion.34
  463.6 5.6 fusion
  470.8 4.6 fusion.1
  475.4 4.2 fusion.112
  479.6 34.5 %reduce-scatter.4.cloned.1.call-done = bf16[1,2,352,1408]{3,2,1,0:T(8,128)(2,1)} async-done(((bf16[1,2,704,1408]{3,2,1,0:T(8,128)(2,1)}), bf16[1,2,352,1408]{3,2,1,0:T(8,128)(2,1)}) %reduce-scatter.4.cloned.1.call-update) | async-done | bytes 1982480 | tf_op jit(solution)/shard_map/reduce_scatter | solution.py:114
  514.1 58.5 %reduce-scatter.6.cloned.1.call-done = bf16[1,1408,768]{2,1,0:T(8,128)(2,1)} async-done(((bf16[1,1408,1536]{2,1,0:T(8,128)(2,1)}), bf16[1,1408,768]{2,1,0:T(8,128)(2,1)}) %reduce-scatter.6.cloned.1.call-update) | async-done | bytes 2162704 | tf_op jit(solution)/shard_map/reduce_scatter | solution.py:117
  572.7 58.7 %reduce-scatter.8.cloned.1.call-done = bf16[1,768,1408]{2,1,0:T(8,128)(2,1)} async-done(((bf16[1,1536,1408]{2,1,0:T(8,128)(2,1)}), bf16[1,768,1408]{2,1,0:T(8,128)(2,1)}) %reduce-scatter.8.cloned.1.call-update) | async-done | bytes 2162704 | tf_op jit(solution)/shard_map/reduce_scatter | solution.py:120
  (135 shorter events, 15.0 us)
Async XLA Ops:
  7.2 1.6 copy-start
  7.2 1.6 copy-start.24
  7.2 63.3 %all-gather.7.cloned.1.call-start = ((), (), s32[]{:S(2)}) async-start(), calls=%async_computation.4 | async-start | bytes 6488064 | tf_op jit(solution)/shard_map/all_gather | solution.py:43
  7.9 1.8 copy-start.23
  7.9 122.3 %all-gather.5.cloned.1.call-start = ((), (), s32[]{:S(2)}) async-start(), calls=%async_computation.3 | async-start | bytes 6488064 | tf_op jit(solution)/shard_map/all_gather | solution.py:44
  8.7 161.8 %all-reduce.5.cloned.1.call-start = ((), (), s32[]{:S(2)}) async-start(), calls=%async_computation.5 | async-start | bytes 1441792 | tf_op jit(solution)/shard_map/psum | solution.py:81
  9.7 64.8 %copy-start.17 = (bf16[128,1408]{1,0:T(8,128)(2,1)}, bf16[128,1408]{1,0:T(8,128)(2,1)S(1)}, u32[]{:S(2)}) copy-start(bf16[128,1408]{1,0:T(8,128)(2,1)S(1)} %gather_fusion.4) | copy-start | bytes 1081348
  70.5 64.5 %slice-start = ((s8[4325376]{0:T(1024)(128)(4,1)}), s8[131072]{0:T(1024)(128)(4,1)S(1)}, s32[]{:S(2)}) async-start(s8[4325376]{0:T(1024)(128)(4,1)} %bitcast.149), calls=%async_computation.14 | async-start | bytes 262144
  130.3 4.8 slice-start.1
  134.3 0.7 copy-start.8
  137.4 88.7 %all-gather.11.cloned.1.call-start = ((), (), s32[]{:S(2)}) async-start(), calls=%async_computation.7 | async-start | bytes 5947392 | tf_op jit(solution)/shard_map/all_gather | solution.py:42
  138.0 111.2 %all-gather.9.cloned.1.call-start = ((), (), s32[]{:S(2)}) async-start(), calls=%async_computation.6 | async-start | bytes 1622016 | tf_op jit(solution)/shard_map/all_gather | solution.py:51
  138.6 173.8 %all-reduce.7.cloned.1.call-start = ((), (), s32[]{:S(2)}) async-start(), calls=%async_computation.8 | async-start | bytes 1441792 | tf_op jit(solution)/shard_map/psum | solution.py:81
  229.5 1.5 collective-permute-start.1
  230.5 28.8 %copy-start.19 = (bf16[128,1408]{1,0:T(8,128)(2,1)}, bf16[128,1408]{1,0:T(8,128)(2,1)S(1)}, u32[]{:S(2)}) copy-start(bf16[128,1408]{1,0:T(8,128)(2,1)S(1)} %gather_fusion.5) | copy-start | bytes 1081348
  230.9 21.0 %collective-permute-start.2 = (bf16[128,704]{0,1:T(8,128)(2,1)S(1)}, bf16[128,704]{0,1:T(8,128)(2,1)S(1)}, u32[]{:S(2)}, u32[]{:S(2)}) collective-permute-start(bf16[128,704]{0,1:T(8,128)(2,1)S(1)} %collective-permute-done.1), channel_id=1, source_target_pairs={{0,8},{4,12},{8,0},{12,4},{16,24},{20,28},{24,16},{28,20},{1,9},{5... | collective-permute-start | bytes 540680 | tf_op jit(solution)/shard_map/ppermute | solution.py:13
  250.7 8.6 %collective-permute-start = (bf16[128,704]{0,1:T(8,128)(2,1)S(1)}, bf16[128,704]{0,1:T(8,128)(2,1)S(1)}, u32[]{:S(2)}, u32[]{:S(2)}) collective-permute-start(bf16[128,704]{0,1:T(8,128)(2,1)S(1)} %get-tuple-element.11), channel_id=1, source_target_pairs={{4,0},{8,4},{12,8},{16,12},{20,16},{24,20},{28,24},{5,1},{9,5},{13... | collective-permute-start | bytes 540680 | tf_op jit(solution)/shard_map/ppermute | solution.py:19
  252.0 14.2 %collective-permute-start.3 = (bf16[128,704]{0,1:T(8,128)(2,1)S(1)}, bf16[128,704]{0,1:T(8,128)(2,1)S(1)}, u32[]{:S(2)}, u32[]{:S(2)}) collective-permute-start(bf16[128,704]{0,1:T(8,128)(2,1)S(1)} %collective-permute-done.2), channel_id=1, source_target_pairs={{0,16},{4,20},{8,24},{12,28},{16,0},{20,4},{24,8},{28,12},{1,17},{... | collective-permute-start | bytes 540680 | tf_op jit(solution)/shard_map/ppermute | solution.py:13
  272.6 5.1 slice-start.2
  272.7 5.0 slice-start.3
  276.9 0.8 copy-start.10
  280.0 103.7 %all-reduce.9.cloned.1.call-start = ((), (), s32[]{:S(2)}) async-start(), calls=%async_computation.9 | async-start | bytes 1441792 | tf_op jit(solution)/shard_map/psum | solution.py:81
  313.6 3.5 copy-start.2
  317.1 1.5 collective-permute-start.5
  318.6 6.6 %collective-permute-start.6 = (bf16[128,704]{0,1:T(8,128)(2,1)S(1)}, bf16[128,704]{0,1:T(8,128)(2,1)S(1)}, u32[]{:S(2)}, u32[]{:S(2)}) collective-permute-start(bf16[128,704]{0,1:T(8,128)(2,1)S(1)} %collective-permute-done.5), channel_id=1, source_target_pairs={{0,8},{4,12},{8,0},{12,4},{16,24},{20,28},{24,16},{28,20},{1,9},{5... | collective-permute-start | bytes 540680 | tf_op jit(solution)/shard_map/ppermute | solution.py:13
  320.9 10.7 %copy-start.21 = (bf16[128,1408]{1,0:T(8,128)(2,1)}, bf16[128,1408]{1,0:T(8,128)(2,1)S(1)}, u32[]{:S(2)}) copy-start(bf16[128,1408]{1,0:T(8,128)(2,1)S(1)} %gather_fusion.6) | copy-start | bytes 1081348
  321.2 10.5 %collective-permute-start.4 = (bf16[128,704]{0,1:T(8,128)(2,1)S(1)}, bf16[128,704]{0,1:T(8,128)(2,1)S(1)}, u32[]{:S(2)}, u32[]{:S(2)}) collective-permute-start(bf16[128,704]{0,1:T(8,128)(2,1)S(1)} %get-tuple-element.9), channel_id=1, source_target_pairs={{4,0},{8,4},{12,8},{16,12},{20,16},{24,20},{28,24},{5,1},{9,5},{13... | collective-permute-start | bytes 540680 | tf_op jit(solution)/shard_map/ppermute | solution.py:19
  325.1 11.5 %collective-permute-start.7 = (bf16[128,704]{0,1:T(8,128)(2,1)S(1)}, bf16[128,704]{0,1:T(8,128)(2,1)S(1)}, u32[]{:S(2)}, u32[]{:S(2)}) collective-permute-start(bf16[128,704]{0,1:T(8,128)(2,1)S(1)} %collective-permute-done.6), channel_id=1, source_target_pairs={{0,16},{4,20},{8,24},{12,28},{16,0},{20,4},{24,8},{28,12},{1,17},{... | collective-permute-start | bytes 540680 | tf_op jit(solution)/shard_map/ppermute | solution.py:13
  343.3 5.1 slice-start.4
  343.4 40.4 %copy-start.3 = (bf16[128,1408]{1,0:T(8,128)(2,1)}, bf16[128,1408]{1,0:T(8,128)(2,1)S(1)}, u32[]{:S(2)}) copy-start(bf16[128,1408]{1,0:T(8,128)(2,1)S(1)} %bitcast_select_fusion.1) | copy-start | bytes 1081348
  343.4 5.0 slice-start.5
  347.6 0.8 copy-start.12
  350.8 104.2 %all-reduce.11.cloned.1.call-start = ((), (), s32[]{:S(2)}) async-start(), calls=%async_computation.10 | async-start | bytes 1441792 | tf_op jit(solution)/shard_map/psum | solution.py:81
  385.0 3.5 copy-start.5
  388.5 1.5 collective-permute-start.9
  389.9 6.6 %collective-permute-start.10 = (bf16[128,704]{0,1:T(8,128)(2,1)S(1)}, bf16[128,704]{0,1:T(8,128)(2,1)S(1)}, u32[]{:S(2)}, u32[]{:S(2)}) collective-permute-start(bf16[128,704]{0,1:T(8,128)(2,1)S(1)} %collective-permute-done.9), channel_id=1, source_target_pairs={{0,8},{4,12},{8,0},{12,4},{16,24},{20,28},{24,16},{28,20},{1,9},{5... | collective-permute-start | bytes 540680 | tf_op jit(solution)/shard_map/ppermute | solution.py:13
  392.3 10.7 %copy-start.22 = (bf16[128,1408]{1,0:T(8,128)(2,1)}, bf16[128,1408]{1,0:T(8,128)(2,1)S(1)}, u32[]{:S(2)}) copy-start(bf16[128,1408]{1,0:T(8,128)(2,1)S(1)} %gather_fusion.7) | copy-start | bytes 1081348
  392.6 10.5 %collective-permute-start.8 = (bf16[128,704]{0,1:T(8,128)(2,1)S(1)}, bf16[128,704]{0,1:T(8,128)(2,1)S(1)}, u32[]{:S(2)}, u32[]{:S(2)}) collective-permute-start(bf16[128,704]{0,1:T(8,128)(2,1)S(1)} %get-tuple-element.7), channel_id=1, source_target_pairs={{4,0},{8,4},{12,8},{16,12},{20,16},{24,20},{28,24},{5,1},{9,5},{13... | collective-permute-start | bytes 540680 | tf_op jit(solution)/shard_map/ppermute | solution.py:19
  396.5 11.5 %collective-permute-start.11 = (bf16[128,704]{0,1:T(8,128)(2,1)S(1)}, bf16[128,704]{0,1:T(8,128)(2,1)S(1)}, u32[]{:S(2)}, u32[]{:S(2)}) collective-permute-start(bf16[128,704]{0,1:T(8,128)(2,1)S(1)} %collective-permute-done.10), channel_id=1, source_target_pairs={{0,16},{4,20},{8,24},{12,28},{16,0},{20,4},{24,8},{28,12},{1,17},{... | collective-permute-start | bytes 540680 | tf_op jit(solution)/shard_map/ppermute | solution.py:13
  414.3 5.3 slice-start.6
  414.6 4.2 copy-start.6
  414.6 5.0 slice-start.7
  418.9 0.7 copy-start.14
  419.6 2.7 copy-start.16
  422.0 92.1 %reduce-scatter.4.cloned.1.call-start = ((), (), s32[]{:S(2)}) async-start(), calls=%async_computation.11 | async-start | bytes 5947392 | tf_op jit(solution)/shard_map/reduce_scatter | solution.py:114
  462.0 1.0 copy-start.9
  462.0 1.1 copy-start.11
  462.0 1.2 copy-start.13
  462.0 1.3 copy-start.15
  462.0 1.4 copy-start.18
  462.0 1.5 copy-start.20
  462.0 110.6 %reduce-scatter.6.cloned.1.call-start = ((), (), s32[]{:S(2)}) async-start(), calls=%async_computation.12 | async-start | bytes 6488064 | tf_op jit(solution)/shard_map/reduce_scatter | solution.py:117
  469.2 1.0 copy-start.4
  469.2 1.1 copy-start.7
  469.2 1.2 copy-start.25
  469.2 1.3 copy-start.26
  469.2 1.4 copy-start.27
  469.2 1.5 copy-start.28
  469.2 162.2 %reduce-scatter.8.cloned.1.call-start = ((), (), s32[]{:S(2)}) async-start(), calls=%async_computation.13 | async-start | bytes 6488064 | tf_op jit(solution)/shard_map/reduce_scatter | solution.py:120
  475.4 156.0 %copy-start.1 = (bf16[1,128,1408]{2,1,0:T(8,128)(2,1)S(1)}, bf16[1,128,1408]{2,1,0:T(8,128)(2,1)}, u32[]{:S(2)}) copy-start(bf16[1,128,1408]{2,1,0:T(8,128)(2,1)} %param.9) | copy-start | bytes 1081348
Sparse Core Ops, SparseCore 0:
  9.5 60.9 all-gather.6
  72.0 58.1 all-gather.4
  137.6 32.9 all-reduce.4
  171.9 54.1 all-gather.10
  227.5 21.6 all-gather.8
  280.2 32.1 all-reduce.6
  350.9 32.8 all-reduce.8
  422.1 32.8 all-reduce.10
  462.2 51.8 reduce-scatter.3
  516.8 55.7 reduce-scatter.5
  575.6 55.7 reduce-scatter.7
where the time goes:
time: 639 us; the launch traced here: 638 us
  waiting for transfers between devices  479 us (75%)
  matrix products  72.9 us (11%)
  blocking collectives  26.9 us (4%)
  local copies, waits for them, and re-layouts  21 us (3%)
  starting transfers between devices  17.4 us (3%)
  between operations  14.5 us (2%)
    psum x4, waiting for transfers between devices, body(): back_mixed = upstream.astype(jnp.float32) + lax.psum(partial_back, 'tensor')  120 us
    reduce_scatter x1, waiting for transfers between devices, body(): lax.psum_scatter(down_total[None].astype(jnp.bfloat16), 'replica', scatte...  58.7 us
    reduce_scatter x1, waiting for transfers between devices, body(): lax.psum_scatter(up_total[None].astype(jnp.bfloat16), 'replica', scatter_...  58.5 us
    all_gather x1, waiting for transfers between devices, body(): lax.all_gather(w_down, 'replica', axis=1, tiled=True)  55.8 us
    all_gather x1, waiting for transfers between devices, body(): lax.all_gather(w_proj, 'replica', axis=2, tiled=True)  54.4 us
    all_gather x1, waiting for transfers between devices, body(): lax.all_gather(w_up, 'replica', axis=2, tiled=True)  52.6 us
    reduce_scatter x1, waiting for transfers between devices, body(): lax.psum_scatter(proj_total[None].astype(jnp.bfloat16), 'replica', scatte...  34.5 us
    ppermute x9, waiting for transfers between devices, from_partner(): return lax.ppermute(value, axis, pairs)  25.6 us
  transfers between devices with their start and end apart: 23, of which 19 were waited for; matrix products, arithmetic and copies ran while one was open for 8% of the time, Pallas kernels for 0%

commit v1 on v0

--- a/solution.py
+++ b/solution.py
@@ -78,7 +78,9 @@
         partial_back = jnp.einsum(
             "mf,df->md", back_hidden, up_local, preferred_element_type=jnp.float32
         )
-        back_mixed = upstream.astype(jnp.float32) + lax.psum(partial_back, "tensor")
+        back_mixed = upstream.astype(jnp.float32) + (
+            partial_back + lax.ppermute(partial_back, "tensor", [(0, 1), (1, 0)])
+        )
         mixed_grad = back_mixed.astype(jnp.bfloat16)
         input_grad = jnp.einsum(
             "mj,kij->mki", mixed_grad, proj_local, preferred_element_type=jnp.float32

time: 639 us -> 538 us (0.84)
  waiting for transfers between devices: 479 us -> 389 us
  matrix products: 72.9 us -> 63 us
    psum x4 -> x0, waiting for transfers between devices: 120 us -> none  [body(): back_mixed = upstream.astype(jnp.float32) + lax.psum(partial_back, 'tensor')]
    ppermute x0 -> x4, waiting for transfers between devices: none -> 52 us  [body(): lax.ppermute(partial_back, 'tensor', [(0, 1), (1, 0)])]
    all_gather x1, waiting for transfers between devices: 54.4 us -> 32.3 us  [body(): lax.all_gather(w_proj, 'replica', axis=2, tiled=True)]
  transfers between devices with their start and end apart: 23 -> 23, of which waited for: 19 -> 19; matrix products, arithmetic and copies ran while one was open for 8% -> 10% of each run, Pallas kernels for 0% -> 0%
where the time goes in v1:
time: 538 us
  waiting for transfers between devices  389 us (72%)
  matrix products  63 us (12%)
  blocking collectives  26.8 us (5%)
  starting transfers between devices  22.9 us (4%)
  local copies, waits for them, and re-layouts  18.6 us (3%)
  between operations  14.9 us (3%)
    reduce_scatter x1, waiting for transfers between devices, body(): lax.psum_scatter(down_total[None].astype(jnp.bfloat16), 'replica', scatte...  58.7 us
    reduce_scatter x1, waiting for transfers between devices, body(): lax.psum_scatter(up_total[None].astype(jnp.bfloat16), 'replica', scatter_...  58.6 us
    all_gather x1, waiting for transfers between devices, body(): lax.all_gather(w_down, 'replica', axis=1, tiled=True)  55.8 us
    ppermute x4, waiting for transfers between devices, body(): lax.ppermute(partial_back, 'tensor', [(0, 1), (1, 0)])  52 us
    all_gather x1, waiting for transfers between devices, body(): lax.all_gather(w_up, 'replica', axis=2, tiled=True)  51.9 us
    reduce_scatter x1, waiting for transfers between devices, body(): lax.psum_scatter(proj_total[None].astype(jnp.bfloat16), 'replica', scatte...  35.5 us
    all_gather x1, waiting for transfers between devices, body(): lax.all_gather(w_proj, 'replica', axis=2, tiled=True)  32.3 us
    ppermute x9, waiting for transfers between devices, from_partner(): return lax.ppermute(value, axis, pairs)  25.7 us
  transfers between devices with their start and end apart: 23, of which 19 were waited for; matrix products, arithmetic and copies ran while one was open for 10% of the time, Pallas kernels for 0%

profile of v1, /device:TPU:0, one launch (start us, length us, event | category | flops | bytes accessed | tf_op | source)
XLA Modules:
  0.0 538.0 jit_solution(15578161076167166799)
XLA Ops:
  8.0 0.7 all-gather.5.cloned.1.call-update
  9.5 0.9 gather_fusion.4
  10.4 8.2 %all_gather.24 = bf16[1,128,1408]{1,2,0:T(8,128)(2,1)S(1)} all-gather(bf16[1,128,704]{1,2,0:T(8,128)(2,1)S(1)} %copy-done.31), channel_id=1, replica_groups=mesh['section'=8,'tensor'=2,'replica'=2] {'tensor'}, dimensions={2}, use_global_device_ids=true | all-gather | bytes 540672 | tf_op jit(solution)/shard_map/all_gather | solution.py:50
  18.6 51.9 %all-gather.7.cloned.1.call-done = bf16[1,1408,1536]{2,1,0:T(8,128)(2,1)} async-done(((bf16[1,1408,768]{2,1,0:T(8,128)(2,1)}), bf16[1,1408,1536]{2,1,0:T(8,128)(2,1)}) %all-gather.7.cloned.1.call-update) | async-done | bytes 4325392 | tf_op jit(solution)/shard_map/all_gather | solution.py:43
  70.5 4.0 multiply_convert_fusion.3
  74.5 55.8 %all-gather.5.cloned.1.call-done = bf16[1,1536,1408]{2,1,0:T(8,128)(2,1)} async-done(((bf16[1,768,1408]{2,1,0:T(8,128)(2,1)}), bf16[1,1536,1408]{2,1,0:T(8,128)(2,1)}) %all-gather.5.cloned.1.call-update) | async-done | bytes 4325392 | tf_op jit(solution)/shard_map/all_gather | solution.py:44
  130.3 4.0 fusion.56
  134.3 1.5 fusion.14
  135.8 1.5 collective-permute-start
  137.7 16.0 %collective-permute-done = f32[128,1408]{1,0:T(8,128)S(1)} collective-permute-done((f32[128,1408]{1,0:T(8,128)S(1)}, f32[128,1408]{1,0:T(8,128)S(1)}, u32[]{:S(2)}, u32[]{:S(2)}) %collective-permute-start) | collective-permute-done | bytes 720928 | tf_op jit(solution)/shard_map/ppermute | solution.py:82
  153.7 32.3 %all-gather.11.cloned.1.call-done = bf16[1,2,704,1408]{3,2,1,0:T(8,128)(2,1)} async-done(((bf16[1,2,352,1408]{3,2,1,0:T(8,128)(2,1)}), bf16[1,2,704,1408]{3,2,1,0:T(8,128)(2,1)}) %all-gather.11.cloned.1.call-update) | async-done | bytes 3964944 | tf_op jit(solution)/shard_map/all_gather | solution.py:42
  186.0 3.3 fusion.100
  189.5 0.9 gather_fusion.5
  190.8 1.5 collective-permute-start.3
  192.3 16.8 %all-gather.9.cloned.1.call-done = bf16[3,128,1408]{1,2,0:T(8,128)(2,1)} async-done(((bf16[3,128,704]{1,2,0:T(8,128)(2,1)}), bf16[3,128,1408]{1,2,0:T(8,128)(2,1)}) %all-gather.9.cloned.1.call-update) | async-done | bytes 1081360 | tf_op jit(solution)/shard_map/all_gather | solution.py:51
  209.1 1.3 fusion.147
  210.6 1.3 collective-permute-start.1
  211.9 3.1 collective-permute-start.4
  215.0 4.2 multiply_convert_fusion.2
  219.1 6.9 %collective-permute-done.4 = bf16[128,704]{0,1:T(8,128)(2,1)S(1)} collective-permute-done((bf16[128,704]{0,1:T(8,128)(2,1)S(1)}, bf16[128,704]{0,1:T(8,128)(2,1)S(1)}, u32[]{:S(2)}, u32[]{:S(2)}) %collective-permute-start.4) | collective-permute-done | bytes 180256 | tf_op jit(solution)/shard_map/ppermute | solution.py:13
  226.1 6.2 %all_gather.29 = bf16[128,1408]{0,1:T(8,128)(2,1)S(1)} all-gather(bf16[128,704]{0,1:T(8,128)(2,1)S(1)} %add_convert_fusion.6), channel_id=1, replica_groups=mesh['section'=8,'tensor'=2,'replica'=2] {'tensor'}, dimensions={1}, use_global_device_ids=true | all-gather | bytes 540672 | tf_op jit(solution)/shard_map/all_gather | solution.py:100
  232.6 4.2 fusion.53
  236.8 1.5 fusion.10
  238.9 14.7 %collective-permute-done.5 = f32[128,1408]{1,0:T(8,128)S(1)} collective-permute-done((f32[128,1408]{1,0:T(8,128)S(1)}, f32[128,1408]{1,0:T(8,128)S(1)}, u32[]{:S(2)}, u32[]{:S(2)}) %collective-permute-start.5) | collective-permute-done | bytes 720928 | tf_op jit(solution)/shard_map/ppermute | solution.py:82
  253.8 1.2 fusion.103
  255.1 1.4 collective-permute-done.7
  256.5 1.7 collective-permute-start.8
  258.3 0.9 gather_fusion.6
  259.4 1.3 collective-permute-start.6
  260.7 2.4 collective-permute-done.8
  263.1 3.4 collective-permute-start.9
  266.5 4.2 multiply_convert_fusion.1
  270.7 5.2 collective-permute-done.9
  276.0 6.3 %all_gather.30 = bf16[128,1408]{0,1:T(8,128)(2,1)S(1)} all-gather(bf16[128,704]{0,1:T(8,128)(2,1)S(1)} %add_convert_fusion.5), channel_id=1, replica_groups=mesh['section'=8,'tensor'=2,'replica'=2] {'tensor'}, dimensions={1}, use_global_device_ids=true | all-gather | bytes 540672 | tf_op jit(solution)/shard_map/all_gather | solution.py:100
  282.6 4.2 fusion.50
  286.9 1.5 fusion.6
  289.0 15.2 %collective-permute-done.10 = f32[128,1408]{1,0:T(8,128)S(1)} collective-permute-done((f32[128,1408]{1,0:T(8,128)S(1)}, f32[128,1408]{1,0:T(8,128)S(1)}, u32[]{:S(2)}, u32[]{:S(2)}) %collective-permute-start.10) | collective-permute-done | bytes 720928 | tf_op jit(solution)/shard_map/ppermute | solution.py:82
  304.4 1.2 fusion.106
  305.7 1.4 collective-permute-done.12
  307.1 1.9 collective-permute-start.13
  309.0 0.9 gather_fusion.7
  310.2 1.3 collective-permute-start.11
  311.5 2.4 collective-permute-done.13
  313.9 3.4 collective-permute-start.14
  317.2 3.9 multiply_convert_fusion
  321.2 5.5 %collective-permute-done.14 = bf16[128,704]{0,1:T(8,128)(2,1)S(1)} collective-permute-done((bf16[128,704]{0,1:T(8,128)(2,1)S(1)}, bf16[128,704]{0,1:T(8,128)(2,1)S(1)}, u32[]{:S(2)}, u32[]{:S(2)}) %collective-permute-start.14) | collective-permute-done | bytes 180256 | tf_op jit(solution)/shard_map/ppermute | solution.py:13
  326.7 6.2 %all_gather.31 = bf16[128,1408]{0,1:T(8,128)(2,1)S(1)} all-gather(bf16[128,704]{0,1:T(8,128)(2,1)S(1)} %add_convert_fusion.4), channel_id=1, replica_groups=mesh['section'=8,'tensor'=2,'replica'=2] {'tensor'}, dimensions={1}, use_global_device_ids=true | all-gather | bytes 540672 | tf_op jit(solution)/shard_map/all_gather | solution.py:100
  333.1 4.0 fusion.47
  337.2 1.5 fusion.2
  340.0 1.4 gather_fusion
  341.4 1.4 gather_fusion.1
  342.8 1.4 gather_fusion.2
  344.2 1.4 gather_fusion.3
  348.5 6.2 %collective-permute-done.15 = f32[128,1408]{1,0:T(8,128)} collective-permute-done((f32[128,1408]{1,0:T(8,128)S(1)}, f32[128,1408]{1,0:T(8,128)}, u32[]{:S(2)}, u32[]{:S(2)}) %collective-permute-start.15) | collective-permute-done | bytes 720928 | tf_op jit(solution)/shard_map/ppermute | solution.py:82
  354.6 1.3 add_convert_fusion
  356.0 4.3 fusion.34
  360.4 0.9 copy-done.17
  361.9 5.5 %fusion = bf16[1,1408,1536]{2,1,0:T(8,128)(2,1)} fusion(bf16[128,1536]{1,0:T(8,128)(2,1)S(1)} %copy-done.23, bf16[128,1536]{1,0:T(8,128)(2,1)S(1)} %copy-done.21, bf16[128,1536]{1,0:T(8,128)(2,1)S(1)} %copy-done.19, bf16[128,1536]{1,0:T(8,128)(2,1)S(1)} %copy-done.17, bf16[128,1408]{1,0:T(8,128)(2,1)} %copy-done.30, bf16[128,1408]{1,0:T(8,128)(2,1)} %copy-done.29, ...), kind=kOutput, calls=%fused_computation.10 | convolution fusion | flops 2228813824 | bytes 7340032 | tf_op jit(solution)/shard_map/md,mf->df/dot_general | solution.py:111
  367.7 0.7 copy-done.7
  369.5 4.6 fusion.1
  374.1 4.1 fusion.112
  378.2 35.5 %reduce-scatter.4.cloned.1.call-done = bf16[1,2,352,1408]{3,2,1,0:T(8,128)(2,1)} async-done(((bf16[1,2,704,1408]{3,2,1,0:T(8,128)(2,1)}), bf16[1,2,352,1408]{3,2,1,0:T(8,128)(2,1)}) %reduce-scatter.4.cloned.1.call-update) | async-done | bytes 1982480 | tf_op jit(solution)/shard_map/reduce_scatter | solution.py:116
  413.8 58.6 %reduce-scatter.6.cloned.1.call-done = bf16[1,1408,768]{2,1,0:T(8,128)(2,1)} async-done(((bf16[1,1408,1536]{2,1,0:T(8,128)(2,1)}), bf16[1,1408,768]{2,1,0:T(8,128)(2,1)}) %reduce-scatter.6.cloned.1.call-update) | async-done | bytes 2162704 | tf_op jit(solution)/shard_map/reduce_scatter | solution.py:119
  472.4 58.7 %reduce-scatter.8.cloned.1.call-done = bf16[1,768,1408]{2,1,0:T(8,128)(2,1)} async-done(((bf16[1,1536,1408]{2,1,0:T(8,128)(2,1)}), bf16[1,768,1408]{2,1,0:T(8,128)(2,1)}) %reduce-scatter.8.cloned.1.call-update) | async-done | bytes 2162704 | tf_op jit(solution)/shard_map/reduce_scatter | solution.py:122
  (147 shorter events, 11.8 us)
Async XLA Ops:
  7.2 2.3 copy-start
  7.2 2.3 copy-start.32
  7.2 63.3 %all-gather.7.cloned.1.call-start = ((), (), s32[]{:S(2)}) async-start(), calls=%async_computation.4 | async-start | bytes 6488064 | tf_op jit(solution)/shard_map/all_gather | solution.py:43
  7.9 122.3 %all-gather.5.cloned.1.call-start = ((), (), s32[]{:S(2)}) async-start(), calls=%async_computation.3 | async-start | bytes 6488064 | tf_op jit(solution)/shard_map/all_gather | solution.py:44
  8.7 1.8 copy-start.31
  8.7 177.3 %all-gather.11.cloned.1.call-start = ((), (), s32[]{:S(2)}) async-start(), calls=%async_computation.6 | async-start | bytes 5947392 | tf_op jit(solution)/shard_map/all_gather | solution.py:42
  9.4 199.6 %all-gather.9.cloned.1.call-start = ((), (), s32[]{:S(2)}) async-start(), calls=%async_computation.5 | async-start | bytes 1622016 | tf_op jit(solution)/shard_map/all_gather | solution.py:51
  10.4 64.1 %copy-start.25 = (bf16[128,1408]{1,0:T(8,128)(2,1)}, bf16[128,1408]{1,0:T(8,128)(2,1)S(1)}, u32[]{:S(2)}) copy-start(bf16[128,1408]{1,0:T(8,128)(2,1)S(1)} %gather_fusion.4) | copy-start | bytes 1081348
  70.5 63.8 %slice-start = ((s8[4325376]{0:T(1024)(128)(4,1)}), s8[131072]{0:T(1024)(128)(4,1)S(1)}, s32[]{:S(2)}) async-start(s8[4325376]{0:T(1024)(128)(4,1)} %bitcast.149), calls=%async_computation.10 | async-start | bytes 262144
  130.3 4.0 slice-start.1
  134.3 1.5 copy-start.16
  135.8 17.8 %collective-permute-start = (f32[128,1408]{1,0:T(8,128)S(1)}, f32[128,1408]{1,0:T(8,128)S(1)}, u32[]{:S(2)}, u32[]{:S(2)}) collective-permute-start(f32[128,1408]{1,0:T(8,128)S(1)} %fusion.14), channel_id=1, source_target_pairs={{0,2},{2,0},{1,3},{3,1},{4,6},{6,4},{5,7},{7,5},{8,10},{10,8},{9,1... | collective-permute-start | bytes 2162696 | tf_op jit(solution)/shard_map/ppermute | solution.py:82
  137.4 276.4 %reduce-scatter.4.cloned.1.call-start = ((), (), s32[]{:S(2)}) async-start(), calls=%async_computation.7 | async-start | bytes 5947392 | tf_op jit(solution)/shard_map/reduce_scatter | solution.py:116
  153.7 36.7 %copy-start.4 = (bf16[128,1408]{1,0:T(8,128)(2,1)}, bf16[128,1408]{1,0:T(8,128)(2,1)S(1)}, u32[]{:S(2)}) copy-start(bf16[128,1408]{1,0:T(8,128)(2,1)S(1)} %add_convert_fusion.3) | copy-start | bytes 1081348
  189.4 1.5 collective-permute-start.2
  190.4 28.8 %copy-start.27 = (bf16[128,1408]{1,0:T(8,128)(2,1)}, bf16[128,1408]{1,0:T(8,128)(2,1)S(1)}, u32[]{:S(2)}) copy-start(bf16[128,1408]{1,0:T(8,128)(2,1)S(1)} %gather_fusion.5) | copy-start | bytes 1081348
  190.8 21.0 %collective-permute-start.3 = (bf16[128,704]{0,1:T(8,128)(2,1)S(1)}, bf16[128,704]{0,1:T(8,128)(2,1)S(1)}, u32[]{:S(2)}, u32[]{:S(2)}) collective-permute-start(bf16[128,704]{0,1:T(8,128)(2,1)S(1)} %collective-permute-done.2), channel_id=1, source_target_pairs={{0,8},{4,12},{8,0},{12,4},{16,24},{20,28},{24,16},{28,20},{1,9},{5... | collective-permute-start | bytes 540680 | tf_op jit(solution)/shard_map/ppermute | solution.py:13
  210.6 8.6 %collective-permute-start.1 = (bf16[128,704]{0,1:T(8,128)(2,1)S(1)}, bf16[128,704]{0,1:T(8,128)(2,1)S(1)}, u32[]{:S(2)}, u32[]{:S(2)}) collective-permute-start(bf16[128,704]{0,1:T(8,128)(2,1)S(1)} %get-tuple-element.11), channel_id=1, source_target_pairs={{4,0},{8,4},{12,8},{16,12},{20,16},{24,20},{28,24},{5,1},{9,5},{13... | collective-permute-start | bytes 540680 | tf_op jit(solution)/shard_map/ppermute | solution.py:19
  211.9 14.2 %collective-permute-start.4 = (bf16[128,704]{0,1:T(8,128)(2,1)S(1)}, bf16[128,704]{0,1:T(8,128)(2,1)S(1)}, u32[]{:S(2)}, u32[]{:S(2)}) collective-permute-start(bf16[128,704]{0,1:T(8,128)(2,1)S(1)} %collective-permute-done.3), channel_id=1, source_target_pairs={{0,16},{4,20},{8,24},{12,28},{16,0},{20,4},{24,8},{28,12},{1,17},{... | collective-permute-start | bytes 540680 | tf_op jit(solution)/shard_map/ppermute | solution.py:13
  232.5 4.3 slice-start.2
  232.6 21.1 %copy-start.6 = (bf16[128,1408]{1,0:T(8,128)(2,1)}, bf16[128,1408]{1,0:T(8,128)(2,1)S(1)}, u32[]{:S(2)}) copy-start(bf16[128,1408]{1,0:T(8,128)(2,1)S(1)} %bitcast_select_fusion.2) | copy-start | bytes 1081348
  232.6 4.2 slice-start.3
  236.8 2.1 copy-start.18
  236.8 17.0 %copy-start.2 = (bf16[1,2,704,1408]{3,2,1,0:T(8,128)(2,1)S(1)}, bf16[1,2,704,1408]{3,2,1,0:T(8,128)(2,1)}, u32[]{:S(2)}) copy-start(bf16[1,2,704,1408]{3,2,1,0:T(8,128)(2,1)} %all-gather.11.cloned.1.call-done) | copy-start | bytes 11894788
  238.4 15.3 %collective-permute-start.5 = (f32[128,1408]{1,0:T(8,128)S(1)}, f32[128,1408]{1,0:T(8,128)S(1)}, u32[]{:S(2)}, u32[]{:S(2)}) collective-permute-start(f32[128,1408]{1,0:T(8,128)S(1)} %fusion.10), channel_id=1, source_target_pairs={{0,2},{2,0},{1,3},{3,1},{4,6},{6,4},{5,7},{7,5},{8,10},{10,8},{9,1... | collective-permute-start | bytes 2162696 | tf_op jit(solution)/shard_map/ppermute | solution.py:82
  253.8 5.4 %copy-start.8 = (bf16[128,1408]{1,0:T(8,128)(2,1)}, bf16[128,1408]{1,0:T(8,128)(2,1)S(1)}, u32[]{:S(2)}) copy-start(bf16[128,1408]{1,0:T(8,128)(2,1)S(1)} %add_convert_fusion.2) | copy-start | bytes 1081348
  255.1 1.5 collective-permute-start.7
  256.5 6.6 %collective-permute-start.8 = (bf16[128,704]{0,1:T(8,128)(2,1)S(1)}, bf16[128,704]{0,1:T(8,128)(2,1)S(1)}, u32[]{:S(2)}, u32[]{:S(2)}) collective-permute-start(bf16[128,704]{0,1:T(8,128)(2,1)S(1)} %collective-permute-done.7), channel_id=1, source_target_pairs={{0,8},{4,12},{8,0},{12,4},{16,24},{20,28},{24,16},{28,20},{1,9},{5... | collective-permute-start | bytes 540680 | tf_op jit(solution)/shard_map/ppermute | solution.py:13
  259.2 11.5 %copy-start.29 = (bf16[128,1408]{1,0:T(8,128)(2,1)}, bf16[128,1408]{1,0:T(8,128)(2,1)S(1)}, u32[]{:S(2)}) copy-start(bf16[128,1408]{1,0:T(8,128)(2,1)S(1)} %gather_fusion.6) | copy-start | bytes 1081348
  259.4 11.3 %collective-permute-start.6 = (bf16[128,704]{0,1:T(8,128)(2,1)S(1)}, bf16[128,704]{0,1:T(8,128)(2,1)S(1)}, u32[]{:S(2)}, u32[]{:S(2)}) collective-permute-start(bf16[128,704]{0,1:T(8,128)(2,1)S(1)} %get-tuple-element.9), channel_id=1, source_target_pairs={{4,0},{8,4},{12,8},{16,12},{20,16},{24,20},{28,24},{5,1},{9,5},{13... | collective-permute-start | bytes 540680 | tf_op jit(solution)/shard_map/ppermute | solution.py:19
  263.1 12.8 %collective-permute-start.9 = (bf16[128,704]{0,1:T(8,128)(2,1)S(1)}, bf16[128,704]{0,1:T(8,128)(2,1)S(1)}, u32[]{:S(2)}, u32[]{:S(2)}) collective-permute-start(bf16[128,704]{0,1:T(8,128)(2,1)S(1)} %collective-permute-done.8), channel_id=1, source_target_pairs={{0,16},{4,20},{8,24},{12,28},{16,0},{20,4},{24,8},{28,12},{1,17},{... | collective-permute-start | bytes 540680 | tf_op jit(solution)/shard_map/ppermute | solution.py:13
  282.5 4.3 slice-start.4
  282.6 21.6 %copy-start.10 = (bf16[128,1408]{1,0:T(8,128)(2,1)}, bf16[128,1408]{1,0:T(8,128)(2,1)S(1)}, u32[]{:S(2)}) copy-start(bf16[128,1408]{1,0:T(8,128)(2,1)S(1)} %bitcast_select_fusion.1) | copy-start | bytes 1081348
  282.6 4.2 slice-start.5
  286.9 2.2 copy-start.20
  286.9 17.5 %copy-start.3 = (bf16[1,2,704,1408]{3,2,1,0:T(8,128)(2,1)S(1)}, bf16[1,2,704,1408]{3,2,1,0:T(8,128)(2,1)}, u32[]{:S(2)}) copy-start(bf16[1,2,704,1408]{3,2,1,0:T(8,128)(2,1)} %all-gather.11.cloned.1.call-done) | copy-start | bytes 11894788
  288.4 15.8 %collective-permute-start.10 = (f32[128,1408]{1,0:T(8,128)S(1)}, f32[128,1408]{1,0:T(8,128)S(1)}, u32[]{:S(2)}, u32[]{:S(2)}) collective-permute-start(f32[128,1408]{1,0:T(8,128)S(1)} %fusion.6), channel_id=1, source_target_pairs={{0,2},{2,0},{1,3},{3,1},{4,6},{6,4},{5,7},{7,5},{8,10},{10,8},{9,1... | collective-permute-start | bytes 2162696 | tf_op jit(solution)/shard_map/ppermute | solution.py:82
  304.4 5.6 %copy-start.12 = (bf16[128,1408]{1,0:T(8,128)(2,1)}, bf16[128,1408]{1,0:T(8,128)(2,1)S(1)}, u32[]{:S(2)}) copy-start(bf16[128,1408]{1,0:T(8,128)(2,1)S(1)} %add_convert_fusion.1) | copy-start | bytes 1081348
  305.6 1.5 collective-permute-start.12
  307.1 6.8 %collective-permute-start.13 = (bf16[128,704]{0,1:T(8,128)(2,1)S(1)}, bf16[128,704]{0,1:T(8,128)(2,1)S(1)}, u32[]{:S(2)}, u32[]{:S(2)}) collective-permute-start(bf16[128,704]{0,1:T(8,128)(2,1)S(1)} %collective-permute-done.12), channel_id=1, source_target_pairs={{0,8},{4,12},{8,0},{12,4},{16,24},{20,28},{24,16},{28,20},{1,9},{5... | collective-permute-start | bytes 540680 | tf_op jit(solution)/shard_map/ppermute | solution.py:13
  309.9 11.2 %copy-start.30 = (bf16[128,1408]{1,0:T(8,128)(2,1)}, bf16[128,1408]{1,0:T(8,128)(2,1)S(1)}, u32[]{:S(2)}) copy-start(bf16[128,1408]{1,0:T(8,128)(2,1)S(1)} %gather_fusion.7) | copy-start | bytes 1081348
  310.2 11.0 %collective-permute-start.11 = (bf16[128,704]{0,1:T(8,128)(2,1)S(1)}, bf16[128,704]{0,1:T(8,128)(2,1)S(1)}, u32[]{:S(2)}, u32[]{:S(2)}) collective-permute-start(bf16[128,704]{0,1:T(8,128)(2,1)S(1)} %get-tuple-element.7), channel_id=1, source_target_pairs={{4,0},{8,4},{12,8},{16,12},{20,16},{24,20},{28,24},{5,1},{9,5},{13... | collective-permute-start | bytes 540680 | tf_op jit(solution)/shard_map/ppermute | solution.py:19
  313.9 12.8 %collective-permute-start.14 = (bf16[128,704]{0,1:T(8,128)(2,1)S(1)}, bf16[128,704]{0,1:T(8,128)(2,1)S(1)}, u32[]{:S(2)}, u32[]{:S(2)}) collective-permute-start(bf16[128,704]{0,1:T(8,128)(2,1)S(1)} %collective-permute-done.13), channel_id=1, source_target_pairs={{0,16},{4,20},{8,24},{12,28},{16,0},{20,4},{24,8},{28,12},{1,17},{... | collective-permute-start | bytes 540680 | tf_op jit(solution)/shard_map/ppermute | solution.py:13
  332.9 4.3 slice-start.6
  333.1 11.1 %copy-start.14 = (bf16[128,1408]{1,0:T(8,128)(2,1)}, bf16[128,1408]{1,0:T(8,128)(2,1)S(1)}, u32[]{:S(2)}) copy-start(bf16[128,1408]{1,0:T(8,128)(2,1)S(1)} %bitcast_select_fusion) | copy-start | bytes 1081348
  333.1 4.0 slice-start.7
  337.2 2.8 copy-start.22
  337.2 2.1 copy-start.24
  338.7 15.9 %collective-permute-start.15 = (f32[128,1408]{1,0:T(8,128)S(1)}, f32[128,1408]{1,0:T(8,128)}, u32[]{:S(2)}, u32[]{:S(2)}) collective-permute-start(f32[128,1408]{1,0:T(8,128)S(1)} %fusion.2), channel_id=1, source_target_pairs={{0,2},{2,0},{1,3},{3,1},{4,6},{6,4},{5,7},{7,5},{8,10},{10,8},{9,1... | collective-permute-start | bytes 2162696 | tf_op jit(solution)/shard_map/ppermute | solution.py:82
  347.5 8.4 %copy-start.5 = (bf16[128,1408]{1,0:T(8,128)(2,1)S(1)}, bf16[128,1408]{1,0:T(8,128)(2,1)}, u32[]{:S(2)}) copy-start(bf16[128,1408]{1,0:T(8,128)(2,1)} %copy-done.4) | copy-start | bytes 1081348
  348.2 7.7 %copy-start.9 = (bf16[128,1408]{1,0:T(8,128)(2,1)S(1)}, bf16[128,1408]{1,0:T(8,128)(2,1)}, u32[]{:S(2)}) copy-start(bf16[128,1408]{1,0:T(8,128)(2,1)} %copy-done.8) | copy-start | bytes 1081348
  348.2 7.7 %copy-start.13 = (bf16[128,1408]{1,0:T(8,128)(2,1)S(1)}, bf16[128,1408]{1,0:T(8,128)(2,1)}, u32[]{:S(2)}) copy-start(bf16[128,1408]{1,0:T(8,128)(2,1)} %copy-done.12) | copy-start | bytes 1081348
  360.3 1.3 copy-start.23
  360.3 1.4 copy-start.26
  360.3 1.5 copy-start.28
  360.3 112.0 %reduce-scatter.6.cloned.1.call-start = ((), (), s32[]{:S(2)}) async-start(), calls=%async_computation.8 | async-start | bytes 6488064 | tf_op jit(solution)/shard_map/reduce_scatter | solution.py:119
  367.4 1.3 copy-start.11
  367.4 1.5 copy-start.15
  367.4 1.6 copy-start.33
  367.4 1.8 copy-start.34
  367.4 1.9 copy-start.35
  367.4 2.0 copy-start.36
  367.4 163.7 %reduce-scatter.8.cloned.1.call-start = ((), (), s32[]{:S(2)}) async-start(), calls=%async_computation.9 | async-start | bytes 6488064 | tf_op jit(solution)/shard_map/reduce_scatter | solution.py:122
  374.1 157.0 %copy-start.1 = (bf16[1,128,1408]{2,1,0:T(8,128)(2,1)S(1)}, bf16[1,128,1408]{2,1,0:T(8,128)(2,1)}, u32[]{:S(2)}) copy-start(bf16[1,128,1408]{2,1,0:T(8,128)(2,1)} %param.9) | copy-start | bytes 1081348
  (4 other events, 4.4 us)
Sparse Core Ops, SparseCore 0:
  9.5 60.9 all-gather.6
  72.0 58.1 all-gather.4
  131.8 54.1 all-gather.10
  187.4 21.6 all-gather.8
  360.5 53.2 reduce-scatter.3
  416.5 55.8 reduce-scatter.5
  475.3 55.7 reduce-scatter.7
